TPU v7x, 256 devices: a whole 4x4x8 slice. The times are simulated.
256 devices in a mesh: seq: 32 (over z, y), mp: 8 (over x, core).
Axes of the slice: x: 4, y: 4, z: 8, core: 2. Of those that a mesh axis runs over, the one named last changes fastest.
Arguments:
- scored_token_targets: int32 [8192], P('seq'), may hold values from 0 to 15999
- valid: int32 [8192], P('seq'), may hold values 0 or 1
- lengths: int32 [48], replicated, may hold values from 1 to 1024, 8192 in all
- owners: int32 [48], replicated, may hold values from 0 to 31
- holders: int32 [48], replicated, may hold values from -1 to 31, as said below
- mixer_input_x: bfloat16 [2, 8192, 3584], P(None, 'seq', 'mp'), may hold values from -6 to 6
- mixer_gate_input: bfloat16 [2, 8192, 3584], P(None, 'seq', 'mp'), may hold values from -6 to 6
- input_projection_b: bfloat16 [2, 8192, 64], P(None, 'seq'), may hold values from -2.390625 to 2.390625
- output_projection_c: bfloat16 [2, 8192, 64], P(None, 'seq'), may hold values from -2.390625 to 2.390625
- token_step_sizes: float32 [2, 8192, 56], P(None, 'seq', 'mp'), may hold values from 0.01 to 0.3
- head_decay_rate: float32 [2, 56], P(None, 'mp'), may hold values from 0.0002 to 1
- head_skip_scale: float32 [2, 56], P(None, 'mp'), may hold values from 0.5 to 1.5
- prompt_held_states: bfloat16 [2, 32, 56, 64, 64], P(None, 'seq', 'mp'), may hold values from -6 to 6
- shared_output_weight: bfloat16 [3584, 3584], P('mp'), may hold values from -0.09375 to 0.09375
- adapter_down_weight: bfloat16 [3584, 128], P('mp'), may hold values from -0.09375 to 0.09375
- adapter_up_weight: bfloat16 [128, 3584], replicated, may hold values from -0.5 to 0.5
- residual: bfloat16 [8192, 2, 3584], P('seq'), may hold values from -16 to 16
- final_norm_scale: float32 [3584], replicated, may hold values from 0.5 to 1.5
- vocab_head_weight: bfloat16 [3584, 16000], P('seq', 'mp'), may hold values from -8 to 8
Outputs:
- owner_sums: float32 [32, 48], P('seq')
- token_delta: float32 [8192], P('seq')
Inputs may be any that keep to these rules, and one draw needn't show every extreme that they name: `holders`: exactly 24 rollouts continue a prompt state; the others start from zeros.
All inputs are finite; a program needn't handle non-finite values. No bound on the sum of `valid` on one device may be relied on, other than what follows from the above.
Results may differ from a plain program's by a relative error of at most 0.035.
Values may be sent and summed in bfloat16 or wider, within the bound.
A program may use at most 128 MiB of HBM per device.

v0:
```python
import jax
import jax.numpy as jnp
from jax import lax
from jax.sharding import PartitionSpec as P

highest = lax.Precision.HIGHEST


def shifted(x, axis, by):
    count = lax.axis_size(axis)
    pairs = [(i, i + by) for i in range(count) if 0 <= i + by < count]
    return lax.ppermute(x, axis, pairs)


def root_norm(hidden, final_norm_scale):
    mean_sq = jnp.mean(hidden * hidden, axis=-1, keepdims=True)
    return (hidden * lax.rsqrt(mean_sq + 1e-05) * final_norm_scale).astype(jnp.bfloat16)


def shards(
    scored_token_targets,
    valid,
    lengths,
    owners,
    holders,
    mixer_input_x,
    mixer_gate_input,
    input_projection_b,
    output_projection_c,
    token_step_sizes,
    head_decay_rate,
    head_skip_scale,
    prompt_held_states,
    shared_output_weight,
    adapter_down_weight,
    adapter_up_weight,
    residual,
    final_norm_scale,
    vocab_head_weight,
):
    seq_count = lax.axis_size("seq")
    mp_count = lax.axis_size("mp")
    tok_rows = scored_token_targets.shape[0]
    models = mixer_input_x.shape[0]
    inner_local = mixer_input_x.shape[2]
    head_count = token_step_sizes.shape[2]
    head_dim = inner_local // head_count
    state_dim = input_projection_b.shape[2]
    roll_count = lengths.shape[0]
    first_row = lax.axis_index("seq") * tok_rows
    offsets = jnp.arange(tok_rows, dtype=jnp.int32)
    position = first_row + offsets
    starts = jnp.cumsum(lengths) - lengths
    rollout = jnp.sum((starts[None, :] <= position[:, None]).astype(jnp.int32), axis=1) - 1
    member_table = rollout[:, None] == jnp.arange(roll_count, dtype=jnp.int32)[None, :]
    start_local = jnp.sum(jnp.where(member_table, starts[None, :], 0), axis=1) - first_row
    holder_tok = jnp.sum(jnp.where(member_table, holders[None, :], 0), axis=1)
    borrowed = (start_local >= 0) & (holder_tok >= 0)
    prompt_pick = (
        (holder_tok[:, None] == jnp.arange(seq_count, dtype=jnp.int32)[None, :]) & borrowed[:, None]
    ).astype(jnp.float32)
    neg_rates = -head_decay_rate
    log_decay = jnp.cumsum(token_step_sizes * neg_rates[:, None, :], axis=1)
    before = jnp.take(log_decay, jnp.maximum(start_local - 1, 0), axis=1)
    before = jnp.where((start_local >= 1)[None, :, None], before, 0.0)
    x_values = mixer_input_x.astype(jnp.float32).reshape(models, tok_rows, head_count, head_dim)
    b_values = input_projection_b.astype(jnp.float32)
    c_values = output_projection_c.astype(jnp.float32)
    gram_matrix = jnp.einsum(
        "mtn,msn->mts", output_projection_c, input_projection_b, preferred_element_type=jnp.float32
    )
    causal = (rollout[:, None] == rollout[None, :]) & (offsets[None, :] <= offsets[:, None])
    log_gap = log_decay[:, :, None, :] - log_decay[:, None, :, :]
    mixing = jnp.where(
        causal[None, :, :, None], jnp.exp(jnp.where(causal[None, :, :, None], log_gap, 0.0)), 0.0
    )
    mixing = mixing * gram_matrix[..., None] * token_step_sizes[:, None, :, :]
    intra_out = jnp.einsum("mtsh,mshp->mthp", mixing, x_values, precision=highest)
    last_pick = prompt_pick[tok_rows - 1]
    zeros_state = jnp.zeros((models, head_count, head_dim, state_dim), jnp.float32)
    piece = lax.all_gather(prompt_held_states, "seq", axis=1, tiled=True)
    last_weight = last_pick.astype(jnp.bfloat16)
    picked = (prompt_pick[None, :, :, None] * c_values[:, :, None, :]).astype(jnp.bfloat16)
    projected = jnp.einsum("mtjn,mjhpn->mthp", picked, piece, preferred_element_type=jnp.float32)
    end_states = jnp.einsum("j,mjhpn->mhpn", last_weight, piece, preferred_element_type=jnp.float32)
    entry_decay = jnp.exp(log_decay - before)
    final_log = log_decay[:, tok_rows - 1, :]
    tail_mask = (rollout == rollout[tok_rows - 1]).astype(jnp.float32)
    end_weight = (
        jnp.exp(final_log[:, None, :] - log_decay) * token_step_sizes * tail_mask[None, :, None]
    )
    local_end = jnp.einsum("msh,mshp,msn->mhpn", end_weight, x_values, b_values, precision=highest)
    local_end = (
        local_end + jnp.exp(final_log - before[:, tok_rows - 1, :])[:, :, None, None] * end_states
    )
    carry_through = jnp.where(start_local[tok_rows - 1] < 0, jnp.exp(final_log), 0.0)

    def relay_step(step_index, incoming):
        outgoing = carry_through[:, :, None, None] * incoming + local_end
        return shifted(outgoing, "seq", 1)

    arriving = lax.fori_loop(0, seq_count - 1, relay_step, zeros_state)
    inherited = (start_local < 0).astype(jnp.float32)
    carried = jnp.einsum("mhpn,mtn->mthp", arriving, c_values, precision=highest)
    carried = carried * (jnp.exp(log_decay) * inherited[None, :, None])[..., None]
    output = (
        intra_out
        + carried
        + entry_decay[..., None] * projected
        + head_skip_scale[:, None, :, None] * x_values
    )
    output = output.reshape(models, tok_rows, inner_local)
    gated_output = (output * jax.nn.silu(mixer_gate_input.astype(jnp.float32))).astype(jnp.bfloat16)
    share_rows = tok_rows // mp_count
    base_output = jnp.einsum(
        "mti,id->tmd", gated_output, shared_output_weight, preferred_element_type=jnp.float32
    )
    low_rank_rows = jnp.dot(
        gated_output[0], adapter_down_weight, preferred_element_type=jnp.float32
    ).astype(jnp.bfloat16)
    adapter_output = jnp.dot(low_rank_rows, adapter_up_weight, preferred_element_type=jnp.float32)
    mixed = lax.psum_scatter(
        jnp.stack([base_output[:, 0] + adapter_output, base_output[:, 1]], axis=1).astype(
            jnp.bfloat16
        ),
        "mp",
        scatter_dimension=0,
        tiled=True,
    ).astype(jnp.float32)
    own_rows = lax.dynamic_slice_in_dim(residual, lax.axis_index("mp") * share_rows, share_rows, 0)
    normed_own = root_norm(own_rows.astype(jnp.float32) + mixed, final_norm_scale)
    normed = lax.all_gather(normed_own, "mp", axis=0, tiled=True)
    vocab_local = vocab_head_weight.shape[1]
    logits = jnp.einsum(
        "tmk,kv->mtv",
        normed,
        lax.all_gather(vocab_head_weight, "seq", axis=0, tiled=True),
        preferred_element_type=jnp.float32,
    )
    vocab_first = lax.axis_index("mp") * vocab_local
    target_hit = (
        scored_token_targets[:, None]
        == vocab_first + jnp.arange(vocab_local, dtype=jnp.int32)[None, :]
    )
    target_local = jnp.sum(jnp.where(target_hit[None], logits, 0.0), axis=2)
    local_max = jnp.max(logits, axis=2)
    vocab_top = lax.pmax(local_max, "mp")
    exp_sums = jnp.sum(jnp.exp(logits - vocab_top[..., None]), axis=2)
    vocab_total, target_logit = lax.psum((exp_sums, target_local), "mp")
    logprob = target_logit - vocab_top - jnp.log(vocab_total)
    token_delta = (logprob[0] - logprob[1]) * valid.astype(jnp.float32)
    roll_sums = jnp.dot(
        token_delta, member_table.astype(jnp.float32), precision=highest
    ) / lengths.astype(jnp.float32)
    owner_rows = (owners[None, :] == jnp.arange(seq_count, dtype=jnp.int32)[:, None]).astype(
        jnp.float32
    ) * roll_sums[None, :]
    owner_sums = lax.psum_scatter(owner_rows, "seq", scatter_dimension=0, tiled=True)
    return (owner_sums, token_delta)


def solution(mesh):
    placed = (
        P("seq"),
        P("seq"),
        P(),
        P(),
        P(),
        P(None, "seq", "mp"),
        P(None, "seq", "mp"),
        P(None, "seq", None),
        P(None, "seq", None),
        P(None, "seq", "mp"),
        P(None, "mp"),
        P(None, "mp"),
        P(None, "seq", "mp", None, None),
        P("mp", None),
        P("mp", None),
        P(),
        P("seq", None, None),
        P(),
        P("seq", "mp"),
    )
    return jax.shard_map(
        shards, mesh=mesh, in_specs=placed, out_specs=(P("seq", None), P("seq")), check_vma=False
    )
```

profile of v0, /device:TPU:0, one launch (start us, length us, event | category | flops | bytes accessed | tf_op | source)
XLA Modules:
  0.0 1076.7 jit_solution(12704770804620089405)
XLA Ops:
  35.8 69.4 %all-gather.4.cloned.1.call-done = bf16[2,32,7,64,64]{4,3,1,2,0:T(8,128)(2,1)} async-done(((bf16[2,1,7,64,64]{4,3,1,2,0:T(8,128)(2,1)}), bf16[2,32,7,64,64]{4,3,1,2,0:T(8,128)(2,1)}) %all-gather.4.cloned.1.call-update) | async-done | bytes 3670032 | tf_op jit(solution)/shard_map/all_gather | solution.py:81
  117.8 498.9 %while.10 = (s32[]{:T(128)}, f32[2,7,64,64]{3,2,1,0:T(8,128)}, f32[2,7]{1,0:T(2,128)S(1)}, f32[2,7,64,64]{3,2,1,0:T(8,128)}, s32[]{:T(128)}) while((s32[]{:T(128)}, f32[2,7,64,64]{3,2,1,0:T(8,128)}, f32[2,7]{1,0:T(2,128)S(1)}, f32[2,7,64,64]{3,2,1,0:T(8,128)}, s32[]{:T(128)}) %tuple.33), condition=%wide.region_7.8_spmd, body=%wide.region_6.7_spmd.sunk | while | flops 114690 | bytes 1605789 | solution.py:102
  122.8 8.9 collective-permute-done
  263.5 8.2 collective-permute-start
  271.7 8.6 collective-permute-done
  282.3 8.2 collective-permute-start
  290.5 9.8 collective-permute-done
  302.4 8.2 collective-permute-start
  310.6 9.9 collective-permute-done
  330.1 8.7 collective-permute-done
  479.0 8.2 collective-permute-start
  487.1 8.2 collective-permute-done
  497.4 8.2 collective-permute-start
  505.6 9.3 collective-permute-done
  517.0 8.2 collective-permute-start
  525.2 10.3 collective-permute-done
  545.1 9.1 collective-permute-done
  637.7 81.4 %reduce-scatter.2.cloned.1.call-done = bf16[32,2,3584]{2,0,1:T(8,128)(2,1)} async-done(((bf16[256,2,3584]{2,0,1:T(8,128)(2,1)}), bf16[32,2,3584]{2,0,1:T(8,128)(2,1)}) %reduce-scatter.2.cloned.1.call-update) | async-done | bytes 458768 | tf_op jit(solution)/shard_map/reduce_scatter | solution.py:122
  725.5 28.5 %all-gather.6.cloned.1.call-done = bf16[256,2,3584]{2,0,1:T(8,128)(2,1)} async-done(((bf16[32,2,3584]{2,0,1:T(8,128)(2,1)}), bf16[256,2,3584]{2,0,1:T(8,128)(2,1)}) %all-gather.6.cloned.1.call-update) | async-done | bytes 3670032 | tf_op jit(solution)/shard_map/all_gather | solution.py:132
  753.9 132.5 %all-gather.8.cloned.1.call-done = bf16[3584,2000]{1,0:T(8,128)(2,1)} async-done(((bf16[112,2000]{1,0:T(8,128)(2,1)}), bf16[3584,2000]{1,0:T(8,128)(2,1)}) %all-gather.8.cloned.1.call-update) | async-done | bytes 14336016 | tf_op jit(solution)/shard_map/all_gather | solution.py:137
  886.4 13.6 %fusion.6 = (f32[2,256]{1,0:T(2,128)S(1)}, f32[2,256]{1,0:T(2,128)S(1)}, f32[256,2,2000]{0,2,1:T(8,128)}) fusion(pred[256,2000]{0,1:T(8,128)(4,1)} %broadcast_compare_fusion, bf16[256,2,3584]{2,0,1:T(8,128)(2,1)} %all-gather.6.cloned.1.call-done, bf16[3584,2000]{1,0:T(8,128)(2,1)} %all-gather.8.cloned.1.call-done), kind=kOutput, calls=%fused_computation.14 | convolution fusion | flops 7343102976 | bytes 22618112 | tf_op jit(solution)/shard_map/tmk,kv->mtv/dot_general | solution.py:134
  900.0 14.3 %pmax.7 = f32[2,256]{1,0:T(2,128)S(1)} all-reduce(f32[2,256]{1,0:T(2,128)S(1)} %get-tuple-element.26), channel_id=1, replica_groups=mesh['seq'=32,'mp'=8] {'mp'}, use_global_device_ids=true, to_apply=%region_13.14 | all-reduce | flops 512 | bytes 4096 | tf_op jit(solution)/shard_map/pmax | solution.py:147
  917.1 12.4 %all-reduce.1 = (f32[2,256]{1,0:T(2,128)S(1)}, f32[2,256]{1,0:T(2,128)S(1)}) all-reduce(f32[2,256]{1,0:T(2,128)S(1)} %fusion.8, f32[2,256]{1,0:T(2,128)S(1)} %get-tuple-element.25), channel_id=1, replica_groups=mesh['seq'=32,'mp'=8] {'mp'}, use_global_device_ids=true, to_apply=%region_15.16 | all-reduce | flops 1024 | bytes 8192 | tf_op jit(solution)/shard_map/psum | solution.py:149
  929.7 139.3 %all-reduce = f32[32,48]{1,0:T(8,128)S(1)} all-reduce(f32[32,48]{1,0:T(8,128)S(1)} %fusion.54), channel_id=3, replica_groups=mesh['seq'=32,'mp'=8] {'seq'}, use_global_device_ids=true, to_apply=%region_16.17.clone | all-reduce | flops 1536 | bytes 12288
  (197 shorter events, 438.7 us)
Async XLA Ops:
  7.2 98.0 %all-gather.4.cloned.1.call-start = ((), (), s32[]{:S(2)}) async-start(), calls=%async_computation.1 | async-start | bytes 7569408 | tf_op jit(solution)/shard_map/all_gather | solution.py:81
  7.9 711.2 %reduce-scatter.2.cloned.1.call-start = ((), (), s32[]{:S(2)}) async-start(), calls=%async_computation.2 | async-start | bytes 4128768 | tf_op jit(solution)/shard_map/reduce_scatter | solution.py:122
  133.7 13.1 %collective-permute-start = (f32[2,7,64,64]{3,2,1,0:T(8,128)}, f32[2,7,64,64]{3,2,1,0:T(8,128)}, u32[]{:S(2)}, u32[]{:S(2)}) collective-permute-start(f32[2,7,64,64]{3,2,1,0:T(8,128)} %multiply_add_fusion.2), channel_id=1, source_target_pairs={{0,8},{8,16},{16,24},{24,32},{32,40},{40,48},{48,56},{56,64},{64,7... | collective-permute-start | bytes 688136 | tf_op jit(solution)/shard_map/while/body/eval_jaxpr/ppermute | solution.py:12
  215.3 12.8 %collective-permute-start = (f32[2,7,64,64]{3,2,1,0:T(8,128)}, f32[2,7,64,64]{3,2,1,0:T(8,128)}, u32[]{:S(2)}, u32[]{:S(2)}) collective-permute-start(f32[2,7,64,64]{3,2,1,0:T(8,128)} %multiply_add_fusion.2), channel_id=1, source_target_pairs={{0,8},{8,16},{16,24},{24,32},{32,40},{40,48},{48,56},{56,64},{64,7... | collective-permute-start | bytes 688136 | tf_op jit(solution)/shard_map/while/body/eval_jaxpr/ppermute | solution.py:12
  230.1 13.9 %collective-permute-start = (f32[2,7,64,64]{3,2,1,0:T(8,128)}, f32[2,7,64,64]{3,2,1,0:T(8,128)}, u32[]{:S(2)}, u32[]{:S(2)}) collective-permute-start(f32[2,7,64,64]{3,2,1,0:T(8,128)} %multiply_add_fusion.2), channel_id=1, source_target_pairs={{0,8},{8,16},{16,24},{24,32},{32,40},{40,48},{48,56},{56,64},{64,7... | collective-permute-start | bytes 688136 | tf_op jit(solution)/shard_map/while/body/eval_jaxpr/ppermute | solution.py:12
  246.1 15.4 %collective-permute-start = (f32[2,7,64,64]{3,2,1,0:T(8,128)}, f32[2,7,64,64]{3,2,1,0:T(8,128)}, u32[]{:S(2)}, u32[]{:S(2)}) collective-permute-start(f32[2,7,64,64]{3,2,1,0:T(8,128)} %multiply_add_fusion.2), channel_id=1, source_target_pairs={{0,8},{8,16},{16,24},{24,32},{32,40},{40,48},{48,56},{56,64},{64,7... | collective-permute-start | bytes 688136 | tf_op jit(solution)/shard_map/while/body/eval_jaxpr/ppermute | solution.py:12
  263.5 16.8 %collective-permute-start = (f32[2,7,64,64]{3,2,1,0:T(8,128)}, f32[2,7,64,64]{3,2,1,0:T(8,128)}, u32[]{:S(2)}, u32[]{:S(2)}) collective-permute-start(f32[2,7,64,64]{3,2,1,0:T(8,128)} %multiply_add_fusion.2), channel_id=1, source_target_pairs={{0,8},{8,16},{16,24},{24,32},{32,40},{40,48},{48,56},{56,64},{64,7... | collective-permute-start | bytes 688136 | tf_op jit(solution)/shard_map/while/body/eval_jaxpr/ppermute | solution.py:12
  282.3 18.0 %collective-permute-start = (f32[2,7,64,64]{3,2,1,0:T(8,128)}, f32[2,7,64,64]{3,2,1,0:T(8,128)}, u32[]{:S(2)}, u32[]{:S(2)}) collective-permute-start(f32[2,7,64,64]{3,2,1,0:T(8,128)} %multiply_add_fusion.2), channel_id=1, source_target_pairs={{0,8},{8,16},{16,24},{24,32},{32,40},{40,48},{48,56},{56,64},{64,7... | collective-permute-start | bytes 688136 | tf_op jit(solution)/shard_map/while/body/eval_jaxpr/ppermute | solution.py:12
  302.4 18.1 %collective-permute-start = (f32[2,7,64,64]{3,2,1,0:T(8,128)}, f32[2,7,64,64]{3,2,1,0:T(8,128)}, u32[]{:S(2)}, u32[]{:S(2)}) collective-permute-start(f32[2,7,64,64]{3,2,1,0:T(8,128)} %multiply_add_fusion.2), channel_id=1, source_target_pairs={{0,8},{8,16},{16,24},{24,32},{32,40},{40,48},{48,56},{56,64},{64,7... | collective-permute-start | bytes 688136 | tf_op jit(solution)/shard_map/while/body/eval_jaxpr/ppermute | solution.py:12
  322.5 16.2 %collective-permute-start = (f32[2,7,64,64]{3,2,1,0:T(8,128)}, f32[2,7,64,64]{3,2,1,0:T(8,128)}, u32[]{:S(2)}, u32[]{:S(2)}) collective-permute-start(f32[2,7,64,64]{3,2,1,0:T(8,128)} %multiply_add_fusion.2), channel_id=1, source_target_pairs={{0,8},{8,16},{16,24},{24,32},{32,40},{40,48},{48,56},{56,64},{64,7... | collective-permute-start | bytes 688136 | tf_op jit(solution)/shard_map/while/body/eval_jaxpr/ppermute | solution.py:12
  340.8 13.8 %collective-permute-start = (f32[2,7,64,64]{3,2,1,0:T(8,128)}, f32[2,7,64,64]{3,2,1,0:T(8,128)}, u32[]{:S(2)}, u32[]{:S(2)}) collective-permute-start(f32[2,7,64,64]{3,2,1,0:T(8,128)} %multiply_add_fusion.2), channel_id=1, source_target_pairs={{0,8},{8,16},{16,24},{24,32},{32,40},{40,48},{48,56},{56,64},{64,7... | collective-permute-start | bytes 688136 | tf_op jit(solution)/shard_map/while/body/eval_jaxpr/ppermute | solution.py:12
  356.7 13.8 %collective-permute-start = (f32[2,7,64,64]{3,2,1,0:T(8,128)}, f32[2,7,64,64]{3,2,1,0:T(8,128)}, u32[]{:S(2)}, u32[]{:S(2)}) collective-permute-start(f32[2,7,64,64]{3,2,1,0:T(8,128)} %multiply_add_fusion.2), channel_id=1, source_target_pairs={{0,8},{8,16},{16,24},{24,32},{32,40},{40,48},{48,56},{56,64},{64,7... | collective-permute-start | bytes 688136 | tf_op jit(solution)/shard_map/while/body/eval_jaxpr/ppermute | solution.py:12
  372.5 12.9 %collective-permute-start = (f32[2,7,64,64]{3,2,1,0:T(8,128)}, f32[2,7,64,64]{3,2,1,0:T(8,128)}, u32[]{:S(2)}, u32[]{:S(2)}) collective-permute-start(f32[2,7,64,64]{3,2,1,0:T(8,128)} %multiply_add_fusion.2), channel_id=1, source_target_pairs={{0,8},{8,16},{16,24},{24,32},{32,40},{40,48},{48,56},{56,64},{64,7... | collective-permute-start | bytes 688136 | tf_op jit(solution)/shard_map/while/body/eval_jaxpr/ppermute | solution.py:12
  431.9 12.8 %collective-permute-start = (f32[2,7,64,64]{3,2,1,0:T(8,128)}, f32[2,7,64,64]{3,2,1,0:T(8,128)}, u32[]{:S(2)}, u32[]{:S(2)}) collective-permute-start(f32[2,7,64,64]{3,2,1,0:T(8,128)} %multiply_add_fusion.2), channel_id=1, source_target_pairs={{0,8},{8,16},{16,24},{24,32},{32,40},{40,48},{48,56},{56,64},{64,7... | collective-permute-start | bytes 688136 | tf_op jit(solution)/shard_map/while/body/eval_jaxpr/ppermute | solution.py:12
  446.8 13.4 %collective-permute-start = (f32[2,7,64,64]{3,2,1,0:T(8,128)}, f32[2,7,64,64]{3,2,1,0:T(8,128)}, u32[]{:S(2)}, u32[]{:S(2)}) collective-permute-start(f32[2,7,64,64]{3,2,1,0:T(8,128)} %multiply_add_fusion.2), channel_id=1, source_target_pairs={{0,8},{8,16},{16,24},{24,32},{32,40},{40,48},{48,56},{56,64},{64,7... | collective-permute-start | bytes 688136 | tf_op jit(solution)/shard_map/while/body/eval_jaxpr/ppermute | solution.py:12
  462.2 14.7 %collective-permute-start = (f32[2,7,64,64]{3,2,1,0:T(8,128)}, f32[2,7,64,64]{3,2,1,0:T(8,128)}, u32[]{:S(2)}, u32[]{:S(2)}) collective-permute-start(f32[2,7,64,64]{3,2,1,0:T(8,128)} %multiply_add_fusion.2), channel_id=1, source_target_pairs={{0,8},{8,16},{16,24},{24,32},{32,40},{40,48},{48,56},{56,64},{64,7... | collective-permute-start | bytes 688136 | tf_op jit(solution)/shard_map/while/body/eval_jaxpr/ppermute | solution.py:12
  479.0 16.4 %collective-permute-start = (f32[2,7,64,64]{3,2,1,0:T(8,128)}, f32[2,7,64,64]{3,2,1,0:T(8,128)}, u32[]{:S(2)}, u32[]{:S(2)}) collective-permute-start(f32[2,7,64,64]{3,2,1,0:T(8,128)} %multiply_add_fusion.2), channel_id=1, source_target_pairs={{0,8},{8,16},{16,24},{24,32},{32,40},{40,48},{48,56},{56,64},{64,7... | collective-permute-start | bytes 688136 | tf_op jit(solution)/shard_map/while/body/eval_jaxpr/ppermute | solution.py:12
  497.4 17.5 %collective-permute-start = (f32[2,7,64,64]{3,2,1,0:T(8,128)}, f32[2,7,64,64]{3,2,1,0:T(8,128)}, u32[]{:S(2)}, u32[]{:S(2)}) collective-permute-start(f32[2,7,64,64]{3,2,1,0:T(8,128)} %multiply_add_fusion.2), channel_id=1, source_target_pairs={{0,8},{8,16},{16,24},{24,32},{32,40},{40,48},{48,56},{56,64},{64,7... | collective-permute-start | bytes 688136 | tf_op jit(solution)/shard_map/while/body/eval_jaxpr/ppermute | solution.py:12
  517.0 18.5 %collective-permute-start = (f32[2,7,64,64]{3,2,1,0:T(8,128)}, f32[2,7,64,64]{3,2,1,0:T(8,128)}, u32[]{:S(2)}, u32[]{:S(2)}) collective-permute-start(f32[2,7,64,64]{3,2,1,0:T(8,128)} %multiply_add_fusion.2), channel_id=1, source_target_pairs={{0,8},{8,16},{16,24},{24,32},{32,40},{40,48},{48,56},{56,64},{64,7... | collective-permute-start | bytes 688136 | tf_op jit(solution)/shard_map/while/body/eval_jaxpr/ppermute | solution.py:12
  537.5 16.7 %collective-permute-start = (f32[2,7,64,64]{3,2,1,0:T(8,128)}, f32[2,7,64,64]{3,2,1,0:T(8,128)}, u32[]{:S(2)}, u32[]{:S(2)}) collective-permute-start(f32[2,7,64,64]{3,2,1,0:T(8,128)} %multiply_add_fusion.2), channel_id=1, source_target_pairs={{0,8},{8,16},{16,24},{24,32},{32,40},{40,48},{48,56},{56,64},{64,7... | collective-permute-start | bytes 688136 | tf_op jit(solution)/shard_map/while/body/eval_jaxpr/ppermute | solution.py:12
  556.3 15.0 %collective-permute-start = (f32[2,7,64,64]{3,2,1,0:T(8,128)}, f32[2,7,64,64]{3,2,1,0:T(8,128)}, u32[]{:S(2)}, u32[]{:S(2)}) collective-permute-start(f32[2,7,64,64]{3,2,1,0:T(8,128)} %multiply_add_fusion.2), channel_id=1, source_target_pairs={{0,8},{8,16},{16,24},{24,32},{32,40},{40,48},{48,56},{56,64},{64,7... | collective-permute-start | bytes 688136 | tf_op jit(solution)/shard_map/while/body/eval_jaxpr/ppermute | solution.py:12
  573.4 13.7 %collective-permute-start = (f32[2,7,64,64]{3,2,1,0:T(8,128)}, f32[2,7,64,64]{3,2,1,0:T(8,128)}, u32[]{:S(2)}, u32[]{:S(2)}) collective-permute-start(f32[2,7,64,64]{3,2,1,0:T(8,128)} %multiply_add_fusion.2), channel_id=1, source_target_pairs={{0,8},{8,16},{16,24},{24,32},{32,40},{40,48},{48,56},{56,64},{64,7... | collective-permute-start | bytes 688136 | tf_op jit(solution)/shard_map/while/body/eval_jaxpr/ppermute | solution.py:12
  635.5 118.4 %all-gather.6.cloned.1.call-start = ((), (), s32[]{:S(2)}) async-start(), calls=%async_computation.3 | async-start | bytes 4128768 | tf_op jit(solution)/shard_map/all_gather | solution.py:132
  722.6 163.8 %all-gather.8.cloned.1.call-start = ((), (), s32[]{:S(2)}) async-start(), calls=%async_computation.4 | async-start | bytes 15138816 | tf_op jit(solution)/shard_map/all_gather | solution.py:137
  (30 other events, 2354.4 us)
Sparse Core Ops, SparseCore 0:
  10.6 94.5 all-gather.3
  635.6 83.3 reduce-scatter.1
  722.7 31.2 all-gather.5
  756.4 129.9 all-gather.7
where the time goes:
time: 1080 us
  waiting for transfers between devices  533 us (49%)
  starting transfers between devices  215 us (20%)
  blocking collectives  166 us (15%)
  other arithmetic  88.2 us (8%)
  matrix products  41 us (4%)
  local copies, waits for them, and re-layouts  18.2 us (2%)
  between operations  14.6 us (1%)
    ppermute x31, waiting for transfers between devices, shifted(): return lax.ppermute(x, axis, pairs)  220 us
    ppermute x31, starting transfers between devices, shifted(): return lax.ppermute(x, axis, pairs)  215 us
    unnamed x1, blocking collectives  139 us
    all_gather x1, waiting for transfers between devices, shards(): lax.all_gather(vocab_head_weight, 'seq', axis=0, tiled=True)  132 us
    reduce_scatter x1, waiting for transfers between devices, shards(): lax.psum_scatter(jnp.stack([base_output[:, 0] + adapter_output, base_outp...  81.4 us
    all_gather x1, waiting for transfers between devices, shards(): piece = lax.all_gather(prompt_held_states, 'seq', axis=1, tiled=True)  69.4 us
    add x31, other arithmetic, relay_step(): outgoing = carry_through[:, :, None, None] * incoming + local_end  63.3 us
    all_gather x1, waiting for transfers between devices, shards(): normed = lax.all_gather(normed_own, 'mp', axis=0, tiled=True)  28.5 us
  transfers between devices with their start and end apart: 35, of which 35 were waited for; matrix products, arithmetic and copies ran while one was open for 3% of the time, Pallas kernels for 0%

commit v1 on v0

--- a/solution.py
+++ b/solution.py
@@ -129,7 +129,9 @@
     ).astype(jnp.float32)
     own_rows = lax.dynamic_slice_in_dim(residual, lax.axis_index("mp") * share_rows, share_rows, 0)
     normed_own = root_norm(own_rows.astype(jnp.float32) + mixed, final_norm_scale)
-    normed = lax.all_gather(normed_own, "mp", axis=0, tiled=True)
+    normed = jnp.concatenate(
+        lax.all_to_all(jnp.stack([normed_own] * lax.axis_size("mp")), "mp", 0, 0), axis=0
+    )
     vocab_local = vocab_head_weight.shape[1]
     logits = jnp.einsum(
         "tmk,kv->mtv",

time: 1080 us -> 1040 us (0.963)
  waiting for transfers between devices: 533 us -> 488 us
    all_gather x1, waiting for transfers between devices: 132 us -> 73.5 us  [shards(): lax.all_gather(vocab_head_weight, 'seq', axis=0, tiled=True)]
    all_to_all x0 -> x1, waiting for transfers between devices: none -> 41.8 us  [shards(): lax.all_to_all(jnp.stack([normed_own] * lax.axis_size('mp')), 'mp', 0, 0)]
    all_gather x1 -> x0, waiting for transfers between devices: 28.5 us -> none  [shards(): normed = lax.all_gather(normed_own, 'mp', axis=0, tiled=True)]
  transfers between devices with their start and end apart: 35 -> 35, of which waited for: 35 -> 35; matrix products, arithmetic and copies ran while one was open for 3% -> 4% of each run, Pallas kernels for 0% -> 0%
where the time goes in v1:
time: 1040 us
  waiting for transfers between devices  488 us (47%)
  starting transfers between devices  220 us (21%)
  blocking collectives  166 us (16%)
  other arithmetic  86.6 us (8%)
  matrix products  40.8 us (4%)
  local copies, waits for them, and re-layouts  24.1 us (2%)
  between operations  14.6 us (1%)
    ppermute x31, waiting for transfers between devices, shifted(): return lax.ppermute(x, axis, pairs)  220 us
    ppermute x31, starting transfers between devices, shifted(): return lax.ppermute(x, axis, pairs)  215 us
    unnamed x1, blocking collectives  139 us
    reduce_scatter x1, waiting for transfers between devices, shards(): lax.psum_scatter(jnp.stack([base_output[:, 0] + adapter_output, base_outp...  81.5 us
    all_gather x1, waiting for transfers between devices, shards(): lax.all_gather(vocab_head_weight, 'seq', axis=0, tiled=True)  73.5 us
    all_gather x1, waiting for transfers between devices, shards(): piece = lax.all_gather(prompt_held_states, 'seq', axis=1, tiled=True)  69.4 us
    add x31, other arithmetic, relay_step(): outgoing = carry_through[:, :, None, None] * incoming + local_end  63.3 us
    all_to_all x1, waiting for transfers between devices, shards(): lax.all_to_all(jnp.stack([normed_own] * lax.axis_size('mp')), 'mp', 0, 0)  41.8 us
  transfers between devices with their start and end apart: 35, of which 35 were waited for; matrix products, arithmetic and copies ran while one was open for 4% of the time, Pallas kernels for 0%

profile of v1, /device:TPU:0, one launch (start us, length us, event | category | flops | bytes accessed | tf_op | source)
XLA Modules:
  0.0 1040.0 jit_solution(1614898430696935011)
XLA Ops:
  35.8 69.4 %all-gather.3.cloned.1.call-done = bf16[2,32,7,64,64]{4,3,1,2,0:T(8,128)(2,1)} async-done(((bf16[2,1,7,64,64]{4,3,1,2,0:T(8,128)(2,1)}), bf16[2,32,7,64,64]{4,3,1,2,0:T(8,128)(2,1)}) %all-gather.3.cloned.1.call-update) | async-done | bytes 3670032 | tf_op jit(solution)/shard_map/all_gather | solution.py:81
  117.8 498.9 %while.10 = (s32[]{:T(128)}, f32[2,7,64,64]{3,2,1,0:T(8,128)}, f32[2,7]{1,0:T(2,128)S(1)}, f32[2,7,64,64]{3,2,1,0:T(8,128)}, s32[]{:T(128)}) while((s32[]{:T(128)}, f32[2,7,64,64]{3,2,1,0:T(8,128)}, f32[2,7]{1,0:T(2,128)S(1)}, f32[2,7,64,64]{3,2,1,0:T(8,128)}, s32[]{:T(128)}) %tuple.33), condition=%wide.region_7.8_spmd, body=%wide.region_6.7_spmd.sunk | while | flops 114690 | bytes 1605789 | solution.py:102
  122.8 8.9 collective-permute-done
  263.5 8.2 collective-permute-start
  271.7 8.6 collective-permute-done
  282.4 8.2 collective-permute-start
  290.5 9.8 collective-permute-done
  302.4 8.2 collective-permute-start
  310.6 9.9 collective-permute-done
  330.1 8.7 collective-permute-done
  479.0 8.2 collective-permute-start
  487.1 8.2 collective-permute-done
  497.4 8.2 collective-permute-start
  505.6 9.3 collective-permute-done
  517.0 8.2 collective-permute-start
  525.2 10.3 collective-permute-done
  545.1 9.1 collective-permute-done
  636.5 81.5 %reduce-scatter.2.cloned.1.call-done = bf16[32,2,3584]{2,0,1:T(8,128)(2,1)} async-done(((bf16[256,2,3584]{2,0,1:T(8,128)(2,1)}), bf16[32,2,3584]{2,0,1:T(8,128)(2,1)}) %reduce-scatter.2.cloned.1.call-update) | async-done | bytes 458768 | tf_op jit(solution)/shard_map/reduce_scatter | solution.py:122
  729.6 41.8 %all-to-all-done = bf16[8,32,2,3584]{3,1,2,0:T(8,128)(2,1)} async-done(((bf16[8,32,2,3584]{3,1,2,0:T(8,128)(2,1)}), bf16[8,32,2,3584]{3,1,2,0:T(8,128)(2,1)}, u32[]{:S(2)}, u32[]{:S(2)}) %all-to-all-start) | async-done | bytes 3670048 | tf_op jit(solution)/shard_map/all_to_all | solution.py:133
  776.0 73.5 %all-gather.5.cloned.1.call-done = bf16[3584,2000]{1,0:T(8,128)(2,1)} async-done(((bf16[112,2000]{1,0:T(8,128)(2,1)}), bf16[3584,2000]{1,0:T(8,128)(2,1)}) %all-gather.5.cloned.1.call-update) | async-done | bytes 14336016 | tf_op jit(solution)/shard_map/all_gather | solution.py:139
  849.6 13.8 %fusion.6 = (f32[2,256]{1,0:T(2,128)S(1)}, f32[2,256]{1,0:T(2,128)S(1)}, f32[256,2,2000]{0,2,1:T(8,128)}) fusion(pred[256,2000]{0,1:T(8,128)(4,1)} %broadcast_compare_fusion, bf16[256,2,3584]{2,0,1:T(8,128)(2,1)} %bitcast.119, bf16[3584,2000]{1,0:T(8,128)(2,1)} %all-gather.5.cloned.1.call-done), kind=kOutput, calls=%fused_computation.14 | convolution fusion | flops 7343102976 | bytes 22618112 | tf_op jit(solution)/shard_map/tmk,kv->mtv/dot_general | solution.py:136
  863.4 14.3 %pmax.7 = f32[2,256]{1,0:T(2,128)S(1)} all-reduce(f32[2,256]{1,0:T(2,128)S(1)} %get-tuple-element.26), channel_id=1, replica_groups=mesh['seq'=32,'mp'=8] {'mp'}, use_global_device_ids=true, to_apply=%region_13.14 | all-reduce | flops 512 | bytes 4096 | tf_op jit(solution)/shard_map/pmax | solution.py:149
  880.4 12.4 %all-reduce.1 = (f32[2,256]{1,0:T(2,128)S(1)}, f32[2,256]{1,0:T(2,128)S(1)}) all-reduce(f32[2,256]{1,0:T(2,128)S(1)} %fusion.8, f32[2,256]{1,0:T(2,128)S(1)} %get-tuple-element.25), channel_id=1, replica_groups=mesh['seq'=32,'mp'=8] {'mp'}, use_global_device_ids=true, to_apply=%region_15.16 | all-reduce | flops 1024 | bytes 8192 | tf_op jit(solution)/shard_map/psum | solution.py:151
  893.0 139.3 %all-reduce = f32[32,48]{1,0:T(8,128)S(1)} all-reduce(f32[32,48]{1,0:T(8,128)S(1)} %fusion.54), channel_id=3, replica_groups=mesh['seq'=32,'mp'=8] {'seq'}, use_global_device_ids=true, to_apply=%region_16.17.clone | all-reduce | flops 1536 | bytes 12288
  (204 shorter events, 447.5 us)
Async XLA Ops:
  7.2 98.0 %all-gather.3.cloned.1.call-start = ((), (), s32[]{:S(2)}) async-start(), calls=%async_computation.2 | async-start | bytes 7569408 | tf_op jit(solution)/shard_map/all_gather | solution.py:81
  7.9 710.1 %reduce-scatter.2.cloned.1.call-start = ((), (), s32[]{:S(2)}) async-start(), calls=%async_computation.3 | async-start | bytes 4128768 | tf_op jit(solution)/shard_map/reduce_scatter | solution.py:122
  133.7 13.1 %collective-permute-start = (f32[2,7,64,64]{3,2,1,0:T(8,128)}, f32[2,7,64,64]{3,2,1,0:T(8,128)}, u32[]{:S(2)}, u32[]{:S(2)}) collective-permute-start(f32[2,7,64,64]{3,2,1,0:T(8,128)} %multiply_add_fusion.2), channel_id=1, source_target_pairs={{0,8},{8,16},{16,24},{24,32},{32,40},{40,48},{48,56},{56,64},{64,7... | collective-permute-start | bytes 688136 | tf_op jit(solution)/shard_map/while/body/eval_jaxpr/ppermute | solution.py:12
  215.3 12.8 %collective-permute-start = (f32[2,7,64,64]{3,2,1,0:T(8,128)}, f32[2,7,64,64]{3,2,1,0:T(8,128)}, u32[]{:S(2)}, u32[]{:S(2)}) collective-permute-start(f32[2,7,64,64]{3,2,1,0:T(8,128)} %multiply_add_fusion.2), channel_id=1, source_target_pairs={{0,8},{8,16},{16,24},{24,32},{32,40},{40,48},{48,56},{56,64},{64,7... | collective-permute-start | bytes 688136 | tf_op jit(solution)/shard_map/while/body/eval_jaxpr/ppermute | solution.py:12
  230.1 13.9 %collective-permute-start = (f32[2,7,64,64]{3,2,1,0:T(8,128)}, f32[2,7,64,64]{3,2,1,0:T(8,128)}, u32[]{:S(2)}, u32[]{:S(2)}) collective-permute-start(f32[2,7,64,64]{3,2,1,0:T(8,128)} %multiply_add_fusion.2), channel_id=1, source_target_pairs={{0,8},{8,16},{16,24},{24,32},{32,40},{40,48},{48,56},{56,64},{64,7... | collective-permute-start | bytes 688136 | tf_op jit(solution)/shard_map/while/body/eval_jaxpr/ppermute | solution.py:12
  246.1 15.4 %collective-permute-start = (f32[2,7,64,64]{3,2,1,0:T(8,128)}, f32[2,7,64,64]{3,2,1,0:T(8,128)}, u32[]{:S(2)}, u32[]{:S(2)}) collective-permute-start(f32[2,7,64,64]{3,2,1,0:T(8,128)} %multiply_add_fusion.2), channel_id=1, source_target_pairs={{0,8},{8,16},{16,24},{24,32},{32,40},{40,48},{48,56},{56,64},{64,7... | collective-permute-start | bytes 688136 | tf_op jit(solution)/shard_map/while/body/eval_jaxpr/ppermute | solution.py:12
  263.5 16.8 %collective-permute-start = (f32[2,7,64,64]{3,2,1,0:T(8,128)}, f32[2,7,64,64]{3,2,1,0:T(8,128)}, u32[]{:S(2)}, u32[]{:S(2)}) collective-permute-start(f32[2,7,64,64]{3,2,1,0:T(8,128)} %multiply_add_fusion.2), channel_id=1, source_target_pairs={{0,8},{8,16},{16,24},{24,32},{32,40},{40,48},{48,56},{56,64},{64,7... | collective-permute-start | bytes 688136 | tf_op jit(solution)/shard_map/while/body/eval_jaxpr/ppermute | solution.py:12
  282.4 18.0 %collective-permute-start = (f32[2,7,64,64]{3,2,1,0:T(8,128)}, f32[2,7,64,64]{3,2,1,0:T(8,128)}, u32[]{:S(2)}, u32[]{:S(2)}) collective-permute-start(f32[2,7,64,64]{3,2,1,0:T(8,128)} %multiply_add_fusion.2), channel_id=1, source_target_pairs={{0,8},{8,16},{16,24},{24,32},{32,40},{40,48},{48,56},{56,64},{64,7... | collective-permute-start | bytes 688136 | tf_op jit(solution)/shard_map/while/body/eval_jaxpr/ppermute | solution.py:12
  302.4 18.1 %collective-permute-start = (f32[2,7,64,64]{3,2,1,0:T(8,128)}, f32[2,7,64,64]{3,2,1,0:T(8,128)}, u32[]{:S(2)}, u32[]{:S(2)}) collective-permute-start(f32[2,7,64,64]{3,2,1,0:T(8,128)} %multiply_add_fusion.2), channel_id=1, source_target_pairs={{0,8},{8,16},{16,24},{24,32},{32,40},{40,48},{48,56},{56,64},{64,7... | collective-permute-start | bytes 688136 | tf_op jit(solution)/shard_map/while/body/eval_jaxpr/ppermute | solution.py:12
  322.5 16.2 %collective-permute-start = (f32[2,7,64,64]{3,2,1,0:T(8,128)}, f32[2,7,64,64]{3,2,1,0:T(8,128)}, u32[]{:S(2)}, u32[]{:S(2)}) collective-permute-start(f32[2,7,64,64]{3,2,1,0:T(8,128)} %multiply_add_fusion.2), channel_id=1, source_target_pairs={{0,8},{8,16},{16,24},{24,32},{32,40},{40,48},{48,56},{56,64},{64,7... | collective-permute-start | bytes 688136 | tf_op jit(solution)/shard_map/while/body/eval_jaxpr/ppermute | solution.py:12
  340.8 13.8 %collective-permute-start = (f32[2,7,64,64]{3,2,1,0:T(8,128)}, f32[2,7,64,64]{3,2,1,0:T(8,128)}, u32[]{:S(2)}, u32[]{:S(2)}) collective-permute-start(f32[2,7,64,64]{3,2,1,0:T(8,128)} %multiply_add_fusion.2), channel_id=1, source_target_pairs={{0,8},{8,16},{16,24},{24,32},{32,40},{40,48},{48,56},{56,64},{64,7... | collective-permute-start | bytes 688136 | tf_op jit(solution)/shard_map/while/body/eval_jaxpr/ppermute | solution.py:12
  356.7 13.8 %collective-permute-start = (f32[2,7,64,64]{3,2,1,0:T(8,128)}, f32[2,7,64,64]{3,2,1,0:T(8,128)}, u32[]{:S(2)}, u32[]{:S(2)}) collective-permute-start(f32[2,7,64,64]{3,2,1,0:T(8,128)} %multiply_add_fusion.2), channel_id=1, source_target_pairs={{0,8},{8,16},{16,24},{24,32},{32,40},{40,48},{48,56},{56,64},{64,7... | collective-permute-start | bytes 688136 | tf_op jit(solution)/shard_map/while/body/eval_jaxpr/ppermute | solution.py:12
  372.5 12.9 %collective-permute-start = (f32[2,7,64,64]{3,2,1,0:T(8,128)}, f32[2,7,64,64]{3,2,1,0:T(8,128)}, u32[]{:S(2)}, u32[]{:S(2)}) collective-permute-start(f32[2,7,64,64]{3,2,1,0:T(8,128)} %multiply_add_fusion.2), channel_id=1, source_target_pairs={{0,8},{8,16},{16,24},{24,32},{32,40},{40,48},{48,56},{56,64},{64,7... | collective-permute-start | bytes 688136 | tf_op jit(solution)/shard_map/while/body/eval_jaxpr/ppermute | solution.py:12
  431.9 12.8 %collective-permute-start = (f32[2,7,64,64]{3,2,1,0:T(8,128)}, f32[2,7,64,64]{3,2,1,0:T(8,128)}, u32[]{:S(2)}, u32[]{:S(2)}) collective-permute-start(f32[2,7,64,64]{3,2,1,0:T(8,128)} %multiply_add_fusion.2), channel_id=1, source_target_pairs={{0,8},{8,16},{16,24},{24,32},{32,40},{40,48},{48,56},{56,64},{64,7... | collective-permute-start | bytes 688136 | tf_op jit(solution)/shard_map/while/body/eval_jaxpr/ppermute | solution.py:12
  446.8 13.4 %collective-permute-start = (f32[2,7,64,64]{3,2,1,0:T(8,128)}, f32[2,7,64,64]{3,2,1,0:T(8,128)}, u32[]{:S(2)}, u32[]{:S(2)}) collective-permute-start(f32[2,7,64,64]{3,2,1,0:T(8,128)} %multiply_add_fusion.2), channel_id=1, source_target_pairs={{0,8},{8,16},{16,24},{24,32},{32,40},{40,48},{48,56},{56,64},{64,7... | collective-permute-start | bytes 688136 | tf_op jit(solution)/shard_map/while/body/eval_jaxpr/ppermute | solution.py:12
  462.2 14.7 %collective-permute-start = (f32[2,7,64,64]{3,2,1,0:T(8,128)}, f32[2,7,64,64]{3,2,1,0:T(8,128)}, u32[]{:S(2)}, u32[]{:S(2)}) collective-permute-start(f32[2,7,64,64]{3,2,1,0:T(8,128)} %multiply_add_fusion.2), channel_id=1, source_target_pairs={{0,8},{8,16},{16,24},{24,32},{32,40},{40,48},{48,56},{56,64},{64,7... | collective-permute-start | bytes 688136 | tf_op jit(solution)/shard_map/while/body/eval_jaxpr/ppermute | solution.py:12
  479.0 16.4 %collective-permute-start = (f32[2,7,64,64]{3,2,1,0:T(8,128)}, f32[2,7,64,64]{3,2,1,0:T(8,128)}, u32[]{:S(2)}, u32[]{:S(2)}) collective-permute-start(f32[2,7,64,64]{3,2,1,0:T(8,128)} %multiply_add_fusion.2), channel_id=1, source_target_pairs={{0,8},{8,16},{16,24},{24,32},{32,40},{40,48},{48,56},{56,64},{64,7... | collective-permute-start | bytes 688136 | tf_op jit(solution)/shard_map/while/body/eval_jaxpr/ppermute | solution.py:12
  497.4 17.5 %collective-permute-start = (f32[2,7,64,64]{3,2,1,0:T(8,128)}, f32[2,7,64,64]{3,2,1,0:T(8,128)}, u32[]{:S(2)}, u32[]{:S(2)}) collective-permute-start(f32[2,7,64,64]{3,2,1,0:T(8,128)} %multiply_add_fusion.2), channel_id=1, source_target_pairs={{0,8},{8,16},{16,24},{24,32},{32,40},{40,48},{48,56},{56,64},{64,7... | collective-permute-start | bytes 688136 | tf_op jit(solution)/shard_map/while/body/eval_jaxpr/ppermute | solution.py:12
  517.0 18.5 %collective-permute-start = (f32[2,7,64,64]{3,2,1,0:T(8,128)}, f32[2,7,64,64]{3,2,1,0:T(8,128)}, u32[]{:S(2)}, u32[]{:S(2)}) collective-permute-start(f32[2,7,64,64]{3,2,1,0:T(8,128)} %multiply_add_fusion.2), channel_id=1, source_target_pairs={{0,8},{8,16},{16,24},{24,32},{32,40},{40,48},{48,56},{56,64},{64,7... | collective-permute-start | bytes 688136 | tf_op jit(solution)/shard_map/while/body/eval_jaxpr/ppermute | solution.py:12
  537.5 16.7 %collective-permute-start = (f32[2,7,64,64]{3,2,1,0:T(8,128)}, f32[2,7,64,64]{3,2,1,0:T(8,128)}, u32[]{:S(2)}, u32[]{:S(2)}) collective-permute-start(f32[2,7,64,64]{3,2,1,0:T(8,128)} %multiply_add_fusion.2), channel_id=1, source_target_pairs={{0,8},{8,16},{16,24},{24,32},{32,40},{40,48},{48,56},{56,64},{64,7... | collective-permute-start | bytes 688136 | tf_op jit(solution)/shard_map/while/body/eval_jaxpr/ppermute | solution.py:12
  556.3 15.0 %collective-permute-start = (f32[2,7,64,64]{3,2,1,0:T(8,128)}, f32[2,7,64,64]{3,2,1,0:T(8,128)}, u32[]{:S(2)}, u32[]{:S(2)}) collective-permute-start(f32[2,7,64,64]{3,2,1,0:T(8,128)} %multiply_add_fusion.2), channel_id=1, source_target_pairs={{0,8},{8,16},{16,24},{24,32},{32,40},{40,48},{48,56},{56,64},{64,7... | collective-permute-start | bytes 688136 | tf_op jit(solution)/shard_map/while/body/eval_jaxpr/ppermute | solution.py:12
  573.4 13.7 %collective-permute-start = (f32[2,7,64,64]{3,2,1,0:T(8,128)}, f32[2,7,64,64]{3,2,1,0:T(8,128)}, u32[]{:S(2)}, u32[]{:S(2)}) collective-permute-start(f32[2,7,64,64]{3,2,1,0:T(8,128)} %multiply_add_fusion.2), channel_id=1, source_target_pairs={{0,8},{8,16},{16,24},{24,32},{32,40},{40,48},{48,56},{56,64},{64,7... | collective-permute-start | bytes 688136 | tf_op jit(solution)/shard_map/while/body/eval_jaxpr/ppermute | solution.py:12
  634.5 215.1 %all-gather.5.cloned.1.call-start = ((), (), s32[]{:S(2)}) async-start(), calls=%async_computation.4 | async-start | bytes 15138816 | tf_op jit(solution)/shard_map/all_gather | solution.py:139
  722.6 48.7 %all-to-all-start = ((bf16[8,32,2,3584]{3,1,2,0:T(8,128)(2,1)}), bf16[8,32,2,3584]{3,1,2,0:T(8,128)(2,1)}, u32[]{:S(2)}, u32[]{:S(2)}) async-start(bf16[8,32,2,3584]{3,1,2,0:T(8,128)(2,1)} %stack.10), calls=%async_computation.1 | async-start | bytes 7340032 | tf_op jit(solution)/shard_map/all_to_all | solution.py:133
  (33 other events, 2374.2 us)
Sparse Core Ops, SparseCore 0:
  10.6 94.5 all-gather.2
  634.6 83.3 reduce-scatter.1
  720.6 128.9 all-gather.4
